TPU v7x, 32 devices: a whole 2x2x4 slice. The times are simulated.
32 devices in a mesh: dp: 16 (over z, x, core), tp: 2 (over y).
Axes of the slice: x: 2, y: 2, z: 4, core: 2. Of those that a mesh axis runs over, the one named last changes fastest.
Arguments:
- tokens: bfloat16 [8192, 768], P('dp'), may hold values from -6 to 6
- neighbours: bfloat16 [128, 128, 768], P('dp'), may hold values from -6 to 6
- out_grad: bfloat16 [8192, 768], P('dp'), may hold values from -6 to 6
- group_sizes: int32 [16], P('dp'), may hold values from 1 to 4, as said below
- seq_lengths: int32 [16, 4], P('dp'), may hold values from 0 to 512, as said below
- stretch_neighbours: int32 [128, 2], P('dp'), may hold values from 0 to 7, as said below
- norm_gain: float32 [3, 768], replicated, may hold values from 0.5 to 1.5
- norm_bias: float32 [3, 768], replicated, may hold values from -1 to 1
- self_qkv_w: bfloat16 [768, 3, 768], P(None, None, 'tp'), may hold values from -0.3125 to 0.3125
- self_qkv_b: float32 [3, 768], P(None, 'tp'), may hold values from -1 to 1
- self_out_w: bfloat16 [768, 768], P('tp'), may hold values from -0.875 to 0.875
- self_out_b: float32 [768], replicated, may hold values from -1 to 1
- cross_q_w: bfloat16 [768, 768], P(None, 'tp'), may hold values from -0.3125 to 0.3125
- cross_q_b: float32 [768], P('tp'), may hold values from -1 to 1
- cross_kv_w: bfloat16 [768, 2, 768], P(None, None, 'tp'), may hold values from -0.3125 to 0.3125
- cross_v_b: float32 [768], P('tp'), may hold values from -1 to 1
- cross_out_w: bfloat16 [768, 768], P('tp'), may hold values from -0.875 to 0.875
- cross_out_b: float32 [768], replicated, may hold values from -1 to 1
- mlp_in_w: bfloat16 [768, 3072], P(None, 'tp'), may hold values from -0.21875 to 0.21875
- mlp_in_b: float32 [3072], P('tp'), may hold values from -1 to 1
- mlp_out_w: bfloat16 [3072, 768], P('tp'), may hold values from -0.21875 to 0.21875
- mlp_out_b: float32 [768], replicated, may hold values from -1 to 1
Outputs:
- output: bfloat16 [8192, 768], P('dp', 'tp')
- tokens_grad: bfloat16 [8192, 768], P('dp', 'tp')
- neighbours_grad: bfloat16 [128, 128, 768], P('dp', None, 'tp')
- norm_gain_grad: float32 [3, 768], replicated
- norm_bias_grad: float32 [3, 768], replicated
- self_qkv_w_grad: float32 [768, 3, 768], P('dp', None, 'tp')
- self_qkv_b_grad: float32 [3, 768], P(None, 'tp')
- self_out_w_grad: float32 [768, 768], P('tp', 'dp')
- self_out_b_grad: float32 [768], replicated
- cross_q_w_grad: float32 [768, 768], P('dp', 'tp')
- cross_q_b_grad: float32 [768], P('tp')
- cross_kv_w_grad: float32 [768, 2, 768], P('dp', None, 'tp')
- cross_v_b_grad: float32 [768], P('tp')
- cross_out_w_grad: float32 [768, 768], P('tp', 'dp')
- cross_out_b_grad: float32 [768], replicated
- mlp_in_w_grad: float32 [768, 3072], P('dp', 'tp')
- mlp_in_b_grad: float32 [3072], P('tp')
- mlp_out_w_grad: float32 [3072, 768], P('tp', 'dp')
- mlp_out_b_grad: float32 [768], replicated
Inputs may be any that keep to these rules, and one draw needn't show every extreme that they name: `group_sizes`: a power of two; bucket b's padded sequence length is 512 // group_sizes[b]; some device has 1 and some has 4 in every draw. `seq_lengths`: slots at or beyond the device's group size are 0; the others lie between a quarter of the padded length and the padded length; the first slot of every device is exactly its padded length. `stretch_neighbours`: indices into the owning device's own 8 stored neighbours; the two of a block differ.
All inputs are finite; a program needn't handle non-finite values.
Results may differ from a plain program's by a relative error of at most 0.024.
The roundings to bfloat16 on the way count: a program that leaves them out, or rounds other values in their place, can miss the bound.
Values sent between devices are 32-bit elements; how exact they have to be, the bound alone decides.
No kernel may reach another device: no remote copies, remote signals or barrier semaphores. Data moves between devices by JAX's collectives and lax.ppermute only.
A program may use at most 192 MiB of HBM per device.

v0:
```python
from functools import partial
import math
import jax
import jax.numpy as jnp
from jax import lax
from jax.sharding import PartitionSpec as P

HEAD_DIM = 64
STRETCH = 64


def norm_forward(field, gain, shift):
    center = field - jnp.mean(field, axis=-1, keepdims=True)
    spread = jnp.mean(center * center, axis=-1, keepdims=True)
    return center * lax.rsqrt(spread + 1e-05) * gain + shift


def norm_backward(field, gain, shift, gradient):
    result, pullback = jax.vjp(norm_forward, field, gain, shift)
    return pullback(gradient)


def exact_gelu(field):
    return jax.nn.gelu(field, approximate=False)


def rotate(field, position, direction):
    halfway = field.shape[-1] // 2
    frequency = jnp.exp(-math.log(10000.0) * jnp.arange(halfway, dtype=jnp.float32) / halfway)
    angles = position.astype(jnp.float32)[:, None] * frequency[None, :]
    cosine = jnp.cos(angles)[:, None, :]
    sine_part = jnp.sin(angles)[:, None, :] * direction
    first_half = field[..., :halfway]
    second_half = field[..., halfway:]
    return jnp.concatenate(
        [
            first_half * cosine - second_half * sine_part,
            second_half * cosine + first_half * sine_part,
        ],
        axis=-1,
    )


def head_scores(query, key_rows, allowed):
    raw_scores = (
        jnp.einsum("qd,kd->qk", query, key_rows, preferred_element_type=jnp.float32) * 0.125
    )
    return jnp.where(allowed, raw_scores, -1e30)


def head_forward(inputs, allowed):
    query, key_rows, value_rows = inputs
    scores = head_scores(query, key_rows, allowed)
    top_score = jnp.max(scores, axis=-1, keepdims=True)
    expo = jnp.exp(scores - top_score)
    total = jnp.sum(expo, axis=-1, keepdims=True)
    probs = (expo / total).astype(jnp.bfloat16)
    mixed = jnp.einsum("qk,kd->qd", probs, value_rows, preferred_element_type=jnp.float32)
    return (mixed, top_score + jnp.log(total))


def head_backward(inputs, allowed):
    query, key_rows, value_rows, row_lse, grad_mix = inputs
    weights = jnp.exp(head_scores(query, key_rows, allowed) - row_lse)
    grad_weights = jnp.einsum("qd,kd->qk", grad_mix, value_rows, preferred_element_type=jnp.float32)
    delta = jnp.sum(weights * grad_weights, axis=-1, keepdims=True)
    grad_scores = (weights * (grad_weights - delta)).astype(jnp.bfloat16)
    grad_query = (
        jnp.einsum("qk,kd->qd", grad_scores, key_rows, preferred_element_type=jnp.float32) * 0.125
    )
    grad_keys = (
        jnp.einsum("qk,qd->kd", grad_scores, query, preferred_element_type=jnp.float32) * 0.125
    )
    grad_values = jnp.einsum(
        "qk,qd->kd", weights.astype(jnp.bfloat16), grad_mix, preferred_element_type=jnp.float32
    )
    return (grad_query, grad_keys, grad_values)


def softmax_parts(scores):
    top_score = jnp.max(scores, axis=-1, keepdims=True)
    expo = jnp.exp(scores - top_score)
    total = jnp.sum(expo, axis=-1, keepdims=True)
    return (expo / total, top_score + jnp.log(total))


def per_device(
    tokens,
    neighbours,
    out_grad,
    group_sizes,
    seq_lengths,
    stretch_neighbours,
    norm_gain,
    norm_bias,
    self_qkv_w,
    self_qkv_b,
    self_out_w,
    self_out_b,
    cross_q_w,
    cross_q_b,
    cross_kv_w,
    cross_v_b,
    cross_out_w,
    cross_out_b,
    mlp_in_w,
    mlp_in_b,
    mlp_out_w,
    mlp_out_b,
):
    count = tokens.shape[0]
    width = tokens.shape[1]
    local = self_qkv_w.shape[2]
    heads = local // HEAD_DIM
    stretches = stretch_neighbours.shape[0]
    stored = neighbours.shape[0]
    span = neighbours.shape[1]
    padded = count // group_sizes[0]
    row_ids = jnp.arange(count, dtype=jnp.int32)
    position = row_ids % padded
    sequence = row_ids // padded
    slot_ids = jnp.arange(seq_lengths.shape[1], dtype=jnp.int32)
    tok_len = jnp.sum(
        jnp.where(sequence[:, None] == slot_ids[None, :], seq_lengths[0][None, :], 0), axis=1
    )
    allowed = (
        (sequence[:, None] == sequence[None, :])
        & (position[None, :] <= position[:, None])
        & (position[None, :] < tok_len[None, :])
    )
    shifted = position + (STRETCH - 1)
    valid = ((shifted < padded) & (shifted < tok_len)).astype(jnp.float32)[:, None]
    resid = tokens.astype(jnp.float32)
    own_width = width // lax.axis_size("tp")
    own_start = lax.axis_index("tp") * own_width
    ln_one = norm_forward(resid, norm_gain[0], norm_bias[0]).astype(jnp.bfloat16)
    qkv_pre = (
        jnp.einsum("td,dcf->tcf", ln_one, self_qkv_w, preferred_element_type=jnp.float32)
        + self_qkv_b
    )
    query = rotate(qkv_pre[:, 0].reshape(count, heads, HEAD_DIM), position, 1.0).astype(
        jnp.bfloat16
    )
    key_rows = rotate(qkv_pre[:, 1].reshape(count, heads, HEAD_DIM), position, 1.0).astype(
        jnp.bfloat16
    )
    value_rows = qkv_pre[:, 2].reshape(count, heads, HEAD_DIM).astype(jnp.bfloat16)
    head_query = jnp.swapaxes(query, 0, 1)
    head_keys = jnp.swapaxes(key_rows, 0, 1)
    head_values = jnp.swapaxes(value_rows, 0, 1)
    head_mix, self_lse = lax.map(
        partial(head_forward, allowed=allowed), (head_query, head_keys, head_values)
    )
    self_mix = jnp.swapaxes(head_mix, 0, 1).reshape(count, local).astype(jnp.bfloat16)
    attn = (
        lax.psum(jnp.dot(self_mix, self_out_w, preferred_element_type=jnp.float32), "tp")
        + self_out_b
    )
    hidden_one = resid + attn
    ln_two = norm_forward(hidden_one, norm_gain[1], norm_bias[1]).astype(jnp.bfloat16)
    cross_query = (
        jnp.dot(ln_two, cross_q_w, preferred_element_type=jnp.float32) + cross_q_b
    ).astype(jnp.bfloat16)
    flat_store = neighbours.reshape(stored * span, width)
    kv_bias = jnp.stack([jnp.zeros_like(cross_v_b), cross_v_b])
    store_kv = (
        jnp.einsum("nd,dcf->ncf", flat_store, cross_kv_w, preferred_element_type=jnp.float32)
        + kv_bias
    ).astype(jnp.bfloat16)
    block_kv = store_kv.reshape(stored, span, 2, heads, HEAD_DIM)[stretch_neighbours].reshape(
        stretches, 2 * span, 2, heads, HEAD_DIM
    )
    block_keys = block_kv[:, :, 0]
    block_values = block_kv[:, :, 1]
    query_rows = jnp.roll(cross_query, -(STRETCH - 1), axis=0).reshape(
        stretches, STRETCH, heads, HEAD_DIM
    )
    cross_scores = (
        jnp.einsum("cqhd,ckhd->chqk", query_rows, block_keys, preferred_element_type=jnp.float32)
        * 0.125
    )
    cross_weights, cross_lse = softmax_parts(cross_scores)
    cross_probs = cross_weights.astype(jnp.bfloat16)
    cross_rows = jnp.einsum(
        "chqk,ckhd->cqhd", cross_probs, block_values, preferred_element_type=jnp.float32
    ).reshape(count, local)
    cross_mix = jnp.roll(cross_rows * valid, STRETCH - 1, axis=0).astype(jnp.bfloat16)
    cross = (
        lax.psum(jnp.dot(cross_mix, cross_out_w, preferred_element_type=jnp.float32), "tp")
        + cross_out_b
    )
    hidden_two = hidden_one + cross
    ln_three = norm_forward(hidden_two, norm_gain[2], norm_bias[2]).astype(jnp.bfloat16)
    pre_act = jnp.dot(ln_three, mlp_in_w, preferred_element_type=jnp.float32) + mlp_in_b
    act, gelu_pull = jax.vjp(exact_gelu, pre_act)
    act_low = act.astype(jnp.bfloat16)
    mlp = (
        lax.psum(jnp.dot(act_low, mlp_out_w, preferred_element_type=jnp.float32), "tp") + mlp_out_b
    )
    output = lax.dynamic_slice_in_dim(hidden_two + mlp, own_start, own_width, 1).astype(
        jnp.bfloat16
    )
    grad_out = out_grad.astype(jnp.float32)
    mlp_out_b_grad = jnp.sum(grad_out, axis=0)
    mlp_out_w_grad = jnp.einsum("tf,td->fd", act_low, out_grad, preferred_element_type=jnp.float32)
    grad_act = jnp.einsum("td,fd->tf", out_grad, mlp_out_w, preferred_element_type=jnp.float32)
    grad_pre = gelu_pull(grad_act)[0].astype(jnp.bfloat16)
    mlp_in_b_grad = jnp.sum(grad_pre.astype(jnp.float32), axis=0)
    mlp_in_w_grad = jnp.einsum("td,tf->df", ln_three, grad_pre, preferred_element_type=jnp.float32)
    grad_ln_three = lax.psum(
        jnp.einsum("tf,df->td", grad_pre, mlp_in_w, preferred_element_type=jnp.float32), "tp"
    )
    grad_in_three, gain_three, shift_three = norm_backward(
        hidden_two, norm_gain[2], norm_bias[2], grad_ln_three
    )
    grad_two = grad_out + grad_in_three
    grad_cross = grad_two.astype(jnp.bfloat16)
    cross_out_b_grad = jnp.sum(grad_cross.astype(jnp.float32), axis=0)
    cross_out_w_grad = jnp.einsum(
        "tf,td->fd", cross_mix, grad_cross, preferred_element_type=jnp.float32
    )
    grad_cross_mix = jnp.einsum(
        "td,fd->tf", grad_cross, cross_out_w, preferred_element_type=jnp.float32
    ).astype(jnp.bfloat16)
    grad_rows = (
        jnp.roll(grad_cross_mix, -(STRETCH - 1), axis=0) * valid.astype(jnp.bfloat16)
    ).reshape(stretches, STRETCH, heads, HEAD_DIM)
    cross_again = jnp.exp(
        jnp.einsum("cqhd,ckhd->chqk", query_rows, block_keys, preferred_element_type=jnp.float32)
        * 0.125
        - cross_lse
    )
    grad_probs = jnp.einsum(
        "cqhd,ckhd->chqk", grad_rows, block_values, preferred_element_type=jnp.float32
    )
    delta = jnp.sum(cross_again * grad_probs, axis=-1, keepdims=True)
    cross_grad_scores = (cross_again * (grad_probs - delta)).astype(jnp.bfloat16)
    grad_query_rows = (
        jnp.einsum(
            "chqk,ckhd->cqhd", cross_grad_scores, block_keys, preferred_element_type=jnp.float32
        )
        * 0.125
    )
    grad_block_keys = (
        jnp.einsum(
            "chqk,cqhd->ckhd", cross_grad_scores, query_rows, preferred_element_type=jnp.float32
        )
        * 0.125
    )
    grad_block_values = jnp.einsum(
        "chqk,cqhd->ckhd", cross_probs, grad_rows, preferred_element_type=jnp.float32
    )
    grad_query = jnp.roll(grad_query_rows.reshape(count, local), STRETCH - 1, axis=0).astype(
        jnp.bfloat16
    )
    cross_q_b_grad = jnp.sum(grad_query.astype(jnp.float32), axis=0)
    cross_q_w_grad = jnp.einsum("td,tf->df", ln_two, grad_query, preferred_element_type=jnp.float32)
    grad_ln_two_part = jnp.einsum(
        "tf,df->td", grad_query, cross_q_w, preferred_element_type=jnp.float32
    )
    grad_block_kv = jnp.stack([grad_block_keys, grad_block_values], axis=2).reshape(
        stretches * 2, span * 2 * local
    )
    owners = (
        stretch_neighbours.reshape(-1)[None, :] == jnp.arange(stored, dtype=jnp.int32)[:, None]
    ).astype(jnp.float32)
    grad_store = (
        jnp.dot(owners, grad_block_kv, precision=lax.Precision.HIGHEST)
        .reshape(stored * span, 2, local)
        .astype(jnp.bfloat16)
    )
    cross_v_b_grad = jnp.sum(grad_store[:, 1].astype(jnp.float32), axis=0)
    cross_kv_w_grad = jnp.einsum(
        "nd,ncf->dcf", flat_store, grad_store, preferred_element_type=jnp.float32
    )
    store_part = jnp.einsum(
        "ncf,dcf->nd", grad_store, cross_kv_w, preferred_element_type=jnp.float32
    ).reshape(stored, span, width)
    neighbours_grad = lax.psum_scatter(store_part, "tp", scatter_dimension=2, tiled=True).astype(
        jnp.bfloat16
    )
    grad_ln_two = lax.psum(grad_ln_two_part, "tp")
    grad_in_two, gain_two, shift_two = norm_backward(
        hidden_one, norm_gain[1], norm_bias[1], grad_ln_two
    )
    grad_one = grad_two + grad_in_two
    grad_attn = grad_one.astype(jnp.bfloat16)
    self_out_b_grad = jnp.sum(grad_attn.astype(jnp.float32), axis=0)
    self_out_w_grad = jnp.einsum(
        "tf,td->fd", self_mix, grad_attn, preferred_element_type=jnp.float32
    )
    grad_self_mix = jnp.einsum(
        "td,fd->tf", grad_attn, self_out_w, preferred_element_type=jnp.float32
    ).astype(jnp.bfloat16)
    head_grad_mix = jnp.swapaxes(grad_self_mix.reshape(count, heads, HEAD_DIM), 0, 1)
    head_dq, head_dk, head_dv = lax.map(
        partial(head_backward, allowed=allowed),
        (head_query, head_keys, head_values, self_lse, head_grad_mix),
    )
    grad_q_rot = rotate(jnp.swapaxes(head_dq, 0, 1), position, -1.0).reshape(count, local)
    grad_k_rot = rotate(jnp.swapaxes(head_dk, 0, 1), position, -1.0).reshape(count, local)
    grad_v_rows = jnp.swapaxes(head_dv, 0, 1).reshape(count, local)
    grad_qkv = jnp.stack([grad_q_rot, grad_k_rot, grad_v_rows], axis=1).astype(jnp.bfloat16)
    self_qkv_b_grad = jnp.sum(grad_qkv.astype(jnp.float32), axis=0)
    self_qkv_w_grad = jnp.einsum(
        "td,tcf->dcf", ln_one, grad_qkv, preferred_element_type=jnp.float32
    )
    grad_ln_one = lax.psum(
        jnp.einsum("tcf,dcf->td", grad_qkv, self_qkv_w, preferred_element_type=jnp.float32), "tp"
    )
    grad_in_one, gain_one, shift_one = norm_backward(resid, norm_gain[0], norm_bias[0], grad_ln_one)
    tokens_grad = lax.dynamic_slice_in_dim(grad_one + grad_in_one, own_start, own_width, 1).astype(
        jnp.bfloat16
    )
    (
        self_qkv_w_grad,
        self_out_w_grad,
        cross_q_w_grad,
        cross_kv_w_grad,
        cross_out_w_grad,
        mlp_in_w_grad,
        mlp_out_w_grad,
    ) = (
        lax.psum_scatter(self_qkv_w_grad, "dp", scatter_dimension=0, tiled=True),
        lax.psum_scatter(self_out_w_grad, "dp", scatter_dimension=1, tiled=True),
        lax.psum_scatter(cross_q_w_grad, "dp", scatter_dimension=0, tiled=True),
        lax.psum_scatter(cross_kv_w_grad, "dp", scatter_dimension=0, tiled=True),
        lax.psum_scatter(cross_out_w_grad, "dp", scatter_dimension=1, tiled=True),
        lax.psum_scatter(mlp_in_w_grad, "dp", scatter_dimension=0, tiled=True),
        lax.psum_scatter(mlp_out_w_grad, "dp", scatter_dimension=1, tiled=True),
    )
    gain_grads = jnp.stack([gain_one, gain_two, gain_three])
    shift_grads = jnp.stack([shift_one, shift_two, shift_three])
    (
        norm_gain_grad,
        norm_bias_grad,
        self_qkv_b_grad,
        self_out_b_grad,
        cross_q_b_grad,
        cross_v_b_grad,
        cross_out_b_grad,
        mlp_in_b_grad,
        mlp_out_b_grad,
    ) = lax.psum(
        (
            gain_grads,
            shift_grads,
            self_qkv_b_grad,
            self_out_b_grad,
            cross_q_b_grad,
            cross_v_b_grad,
            cross_out_b_grad,
            mlp_in_b_grad,
            mlp_out_b_grad,
        ),
        "dp",
    )
    return (
        output,
        tokens_grad,
        neighbours_grad,
        norm_gain_grad,
        norm_bias_grad,
        self_qkv_w_grad,
        self_qkv_b_grad,
        self_out_w_grad,
        self_out_b_grad,
        cross_q_w_grad,
        cross_q_b_grad,
        cross_kv_w_grad,
        cross_v_b_grad,
        cross_out_w_grad,
        cross_out_b_grad,
        mlp_in_w_grad,
        mlp_in_b_grad,
        mlp_out_w_grad,
        mlp_out_b_grad,
    )


def solution(mesh):
    placed = (
        P("dp", None),
        P("dp", None, None),
        P("dp", None),
        P("dp"),
        P("dp", None),
        P("dp", None),
        P(),
        P(),
        P(None, None, "tp"),
        P(None, "tp"),
        P("tp", None),
        P(),
        P(None, "tp"),
        P("tp"),
        P(None, None, "tp"),
        P("tp"),
        P("tp", None),
        P(),
        P(None, "tp"),
        P("tp"),
        P("tp", None),
        P(),
    )
    return jax.shard_map(
        per_device,
        mesh=mesh,
        in_specs=placed,
        out_specs=(
            P("dp", "tp"),
            P("dp", "tp"),
            P("dp", None, "tp"),
            P(),
            P(),
            P("dp", None, "tp"),
            P(None, "tp"),
            P("tp", "dp"),
            P(),
            P("dp", "tp"),
            P("tp"),
            P("dp", None, "tp"),
            P("tp"),
            P("tp", "dp"),
            P(),
            P("dp", "tp"),
            P("tp"),
            P("tp", "dp"),
            P(),
        ),
        check_vma=False,
    )
```

profile of v0, /device:TPU:0, one launch (start us, length us, event | category | flops | bytes accessed | tf_op | source)
XLA Modules:
  0.0 986.2 jit_solution(2578824090523314707)
XLA Ops:
  11.8 2.8 convolution_add_fusion.1
  20.6 2.4 subtract_convert_fusion.2
  24.2 2.2 copy.158
  28.2 2.2 copy.159
  30.4 20.7 %while.30 = (s32[]{:T(128)}, bf16[6,512,64]{1,2,0:T(8,128)(2,1)S(1)}, f32[6,512,1]{1,2,0:T(1,128)}, bf16[6,512,64]{2,1,0:T(8,128)(2,1)}, bf16[6,512,64]{2,1,0:T(...) while((s32[]{:T(128)}, ...), condition=%wide.region_6.7_spmd.clone.clone, body=%wide.region_3.6_spmd.clone.sunk.clone | while | flops 70254080 | bytes 3701353 | solution.py:151
  51.1 3.1 fusion.123
  55.1 4.3 add_convert_fusion.1
  59.4 2.7 copy.162
  62.2 2.0 copy.197
  65.8 4.0 gather_fusion
  69.8 6.0 copy.165
  75.8 5.6 reshape.384
  81.5 3.8 fusion.120
  85.3 23.3 %all-reduce.11.cloned.1.call-done = f32[512,768]{1,0:T(8,128)} async-done(((f32[512,768]{1,0:T(8,128)}), f32[512,768]{1,0:T(8,128)}) %all-reduce.11.cloned.1.call-update) | async-done | bytes 1572880 | tf_op jit(solution)/shard_map/psum | solution.py:156
  114.5 2.3 copy.181
  116.8 2.8 multiply_reduce_fusion.2
  122.2 2.4 convolution_bitcast_fusion.6
  124.6 2.1 copy.170
  126.6 2.6 reshape.386
  131.3 2.0 fusion.82
  134.4 50.7 %all-reduce.13.cloned.1.call-done = f32[512,768]{1,0:T(8,128)} async-done(((f32[512,768]{1,0:T(8,128)}), f32[512,768]{1,0:T(8,128)}) %all-reduce.13.cloned.1.call-update) | async-done | bytes 1572880 | tf_op jit(solution)/shard_map/psum | solution.py:189
  185.0 2.3 fusion.117
  190.1 10.2 %convert_reduce_fusion = (f32[1536]{0:T(1024)}, bf16[512,1536]{1,0:T(8,128)(2,1)S(1)}, f32[512,1536]{1,0:T(8,128)}) fusion(f32[512,1536]{1,0:T(8,128)S(1)} %convolution_add_fusion, bf16[512,768]{1,0:T(8,128)(2,1)S(1)} %copy-done.17, bf16[1536,768]{1,0:T(8,128)(2,1)S(1)} %copy-done), kind=kOutput, calls=%fused_computation.61 | convolution fusion | flops 1266153984 | bytes 11016192 | tf_op jit(solution)/shard_map/td,fd->tf/dot_general | solution.py:206
  201.5 2.6 fusion.125
  205.5 3.6 multiply_convert_fusion.2
  210.2 2.5 fusion.124
  212.7 43.0 %all-reduce.15.cloned.1.call-done = f32[512,768]{1,0:T(8,128)} async-done(((f32[512,768]{1,0:T(8,128)}), f32[512,768]{1,0:T(8,128)}) %all-reduce.15.cloned.1.call-update) | async-done | bytes 1572880 | tf_op jit(solution)/shard_map/psum | solution.py:210
  255.8 3.2 multiply_reduce_fusion.3
  264.7 3.7 multiply_reduce_fusion.1
  271.0 2.2 multiply_bitcast_fusion
  277.3 3.8 convolution_bitcast_fusion.2
  281.1 3.4 pad_maximum_fusion
  284.5 13.7 %copy.183 = f32[8,256,2,6,64]{4,3,2,1,0:T(8,128)} copy(f32[8,256,2,6,64]{1,4,3,0,2:T(8,128)} %pad_maximum_fusion) | data formatting | bytes 12582912 | tf_op jit(solution)/shard_map/stack | solution.py:261
  298.1 14.9 %reshape.389 = f32[16,98304]{1,0:T(8,128)} reshape(f32[8,256,2,6,64]{4,3,2,1,0:T(8,128)} %copy.183) | data formatting | bytes 12582912 | tf_op jit(solution)/shard_map/reshape | solution.py:261
  313.1 6.3 convolution_convert_fusion
  319.4 2.7 convert_element_type.173
  322.1 4.9 convolution_bitcast_fusion.4
  327.0 5.3 copy.188
  333.7 2.7 multiply_reduce_fusion.4
  341.5 57.1 %while.31 = (s32[]{:T(128)}, f32[6,512,64]{1,2,0:T(8,128)}, f32[6,512,64]{1,2,0:T(8,128)}, bf16[6,512,64]{1,2,0:T(8,128)(2,1)}, bf16[6,512,64]{2,1,0:T(8,128)(2,...) while((s32[]{:T(128)}, f32[6,512,64]{1,2,0:T(8,128)}, ...), condition=%wide.region_25.26_spmd.clone.clone, body=%wide.region_23.25_spmd.clone.sunk.clone | while | flops 171245056 | bytes 12345017 | solution.py:296
  347.3 2.0 fusion.206
  356.8 2.0 fusion.206
  366.3 2.0 fusion.206
  375.8 2.0 fusion.206
  385.4 2.0 fusion.206
  394.9 2.0 fusion.206
  402.2 4.0 convolution_bitcast_fusion.5
  407.7 4.5 convolution_bitcast_fusion.3
  417.1 3.2 fusion.108
  420.4 5.2 fusion.111
  426.7 5.0 fusion.126
  432.7 4.4 fusion.78
  439.5 3.6 fusion.62
  445.9 72.7 %all-reduce.21.cloned.1.call-done = (f32[512,768]{1,0:T(8,128)}, f32[512,768]{1,0:T(8,128)}) async-done(((f32[512,768]{1,0:T(8,128)}, f32[512,768]{1,0:T(8,128)}), (f32[512,768]{1,0:T(8,128)}, f32[512,768]{1,0:T(8,128)})) %all-reduce.21.cloned.1.call-update) | async-done | bytes 3145744 | tf_op jit(solution)/shard_map/psum | solution.py:198
  518.6 2.1 fusion.59
  520.8 61.8 %all-reduce.2 = (f32[3,768]{1,0:T(4,128)}, f32[3,768]{1,0:T(4,128)}, f32[3,384]{1,0:T(4,128)}, f32[768]{0:T(1024)}, f32[384]{0:T(512)}, /*index=5*/f32[384]{0:T(...) all-reduce(f32[3,768]{1,0:T(4,128)S(1)} %pad_maximum_fusion.12, ...), channel_id=1, replica_groups=mesh['dp'=16,'tp'=2] {'dp'}, use_global_device_ids=true, to_apply=%region_33.34 | all-reduce | flops 10368 | bytes 82944 | tf_op jit(solution)/shard_map/psum | solution.py:344
  582.6 2.2 fusion.114
  587.3 2.4 convert_element_type.169
  589.7 37.0 %reduce-scatter.16.cloned.1.call-done = f32[384,48]{0,1:T(8,128)} async-done(((f32[384,768]{0,1:T(8,128)}), f32[384,48]{0,1:T(8,128)}) %reduce-scatter.16.cloned.1.call-update) | async-done | bytes 73744 | tf_op jit(solution)/shard_map/reduce_scatter | solution.py:328
  626.7 61.4 %reduce-scatter.14.cloned.1.call-done = f32[48,384]{1,0:T(8,128)} async-done(((f32[768,384]{1,0:T(8,128)}), f32[48,384]{1,0:T(8,128)}) %reduce-scatter.14.cloned.1.call-update) | async-done | bytes 73744 | tf_op jit(solution)/shard_map/reduce_scatter | solution.py:326
  688.2 61.3 %reduce-scatter.12.cloned.1.call-done = f32[384,48]{0,1:T(8,128)} async-done(((f32[384,768]{0,1:T(8,128)}), f32[384,48]{0,1:T(8,128)}) %reduce-scatter.12.cloned.1.call-update) | async-done | bytes 73744 | tf_op jit(solution)/shard_map/reduce_scatter | solution.py:325
  749.4 79.0 %reduce-scatter.18.cloned.1.call-done = f32[48,1536]{1,0:T(8,128)} async-done(((f32[768,1536]{1,0:T(8,128)}), f32[48,1536]{1,0:T(8,128)}) %reduce-scatter.18.cloned.1.call-update) | async-done | bytes 294928 | tf_op jit(solution)/shard_map/reduce_scatter | solution.py:329
  828.5 79.1 %reduce-scatter.20.cloned.1.call-done = f32[1536,48]{0,1:T(8,128)} async-done(((f32[1536,768]{0,1:T(8,128)}), f32[1536,48]{0,1:T(8,128)}) %reduce-scatter.20.cloned.1.call-update) | async-done | bytes 294928 | tf_op jit(solution)/shard_map/reduce_scatter | solution.py:330
  907.5 71.9 %reduce-scatter.10.cloned.1.call-done = f32[48,3,384]{2,0,1:T(8,128)} async-done(((f32[768,3,384]{2,0,1:T(8,128)}), f32[48,3,384]{2,0,1:T(8,128)}) %reduce-scatter.10.cloned.1.call-update) | async-done | bytes 221200 | tf_op jit(solution)/shard_map/reduce_scatter | solution.py:324
  (436 shorter events, 135.9 us)
Async XLA Ops:
  7.2 182.9 %copy-start = (bf16[1536,768]{1,0:T(8,128)(2,1)S(1)}, bf16[1536,768]{1,0:T(8,128)(2,1)}, u32[]{:S(2)}) copy-start(bf16[1536,768]{1,0:T(8,128)(2,1)} %param.46) | copy-start | bytes 7077892
  7.2 3.0 copy-start.9
  7.2 101.4 %all-reduce.11.cloned.1.call-start = ((), (), s32[]{:S(2)}) async-start(), calls=%async_computation.7 | async-start | bytes 3145728 | tf_op jit(solution)/shard_map/psum | solution.py:156
  8.6 3.1 copy-start.108
  8.7 10.3 %copy-start.29 = (bf16[6,512,64]{1,2,0:T(8,128)(2,1)}, bf16[6,512,64]{1,2,0:T(8,128)(2,1)S(1)}, u32[]{:S(2)}) copy-start(bf16[6,512,64]{1,2,0:T(8,128)(2,1)S(1)} %fusion.122) | copy-start | bytes 1179652
  10.2 4.5 copy-start.68
  11.1 3.5 copy-start.74
  11.8 2.9 copy-start.66
  11.8 2.9 copy-start.97
  24.2 6.2 copy-start.34
  24.2 6.2 copy-start.90
  51.1 3.1 copy-start.32
  51.1 3.8 copy-start.95
  54.2 130.8 %all-reduce.13.cloned.1.call-start = ((), (), s32[]{:S(2)}) async-start(), calls=%async_computation.8 | async-start | bytes 3145728 | tf_op jit(solution)/shard_map/psum | solution.py:189
  81.5 27.2 %copy-start.101 = (f32[768]{0:T(1024)S(1)}, f32[768]{0:T(1024)}, u32[]{:S(2)}) copy-start(f32[768]{0:T(1024)} %param.37) | copy-start | bytes 9220
  119.6 85.2 %copy-start.60 = (f32[8,6,64]{2,1,0:T(8,128)}, f32[8,6,64]{2,1,0:T(8,128)S(1)}, u32[]{:S(2)}) copy-start(f32[8,6,64]{2,1,0:T(8,128)S(1)} %get-tuple-element.443) | copy-start | bytes 36868
  120.7 84.1 %copy-start.64 = (f32[8,6,64]{2,1,0:T(8,128)}, f32[8,6,64]{2,1,0:T(8,128)S(1)}, u32[]{:S(2)}) copy-start(f32[8,6,64]{2,1,0:T(8,128)S(1)} %fusion.50) | copy-start | bytes 36868
  126.6 2.6 copy-start.87
  131.3 53.7 %copy-start.94 = (f32[768]{0:T(1024)S(1)}, f32[768]{0:T(1024)}, u32[]{:S(2)}) copy-start(f32[768]{0:T(1024)} %param.43) | copy-start | bytes 9220
  133.3 122.4 %all-reduce.15.cloned.1.call-start = ((), (), s32[]{:S(2)}) async-start(), calls=%async_computation.9 | async-start | bytes 3145728 | tf_op jit(solution)/shard_map/psum | solution.py:210
  185.0 3.5 copy-start.106
  187.7 71.3 %copy-start.76 = (f32[512]{0:T(512)}, f32[512]{0:T(512)S(1)}, u32[]{:S(2)}) copy-start(f32[512]{0:T(512)S(1)} %fusion.101) | copy-start | bytes 6148
  190.1 10.2 %copy-start.37 = (f32[512,1536]{1,0:T(8,128)}, f32[512,1536]{1,0:T(8,128)S(1)}, u32[]{:S(2)}) copy-start(f32[512,1536]{1,0:T(8,128)S(1)} %convolution_add_fusion) | copy-start | bytes 9437188
  204.1 128.5 %all-reduce.17.cloned.1.call-start = ((), (), s32[]{:S(2)}) async-start(), calls=%async_computation.10 | async-start | bytes 3145728 | tf_op jit(solution)/shard_map/psum | solution.py:282
  212.7 46.2 %copy-start.7 = (f32[512,768]{1,0:T(8,128)S(1)}, f32[512,768]{1,0:T(8,128)}, u32[]{:S(2)}) copy-start(f32[512,768]{1,0:T(8,128)} %copy-done.6) | copy-start | bytes 4718596
  255.8 3.2 copy-start.23
  264.7 3.7 copy-start.35
  264.7 3.7 copy-start.5
  276.8 166.3 %all-reduce.19.cloned.1.call-start = ((), (), s32[]{:S(2)}) async-start(), calls=%async_computation.18 | async-start | bytes 4718592
  277.3 3.8 copy-start.14
  298.1 14.9 %copy-start.102 = (s32[16]{0:T(128)S(1)}, s32[16]{0:T(128)}, u32[]{:S(2)}) copy-start(s32[16]{0:T(128)} %eq.52) | copy-start | bytes 196
  322.1 4.9 copy-start.20
  332.4 186.2 %all-reduce.21.cloned.1.call-start = ((), (), s32[]{:S(2)}) async-start(), calls=%async_computation.19 | async-start | bytes 6291456 | tf_op jit(solution)/shard_map/psum | solution.py:198
  333.7 3.4 copy-start.22
  341.5 58.4 %copy-start.54 = (f32[512,32]{0,1:T(8,128)S(1)}, f32[512,32]{0,1:T(8,128)}, u32[]{:S(2)}) copy-start(f32[512,32]{0,1:T(8,128)} %copy-done.53) | copy-start | bytes 196612
  341.5 58.4 %copy-start.63 = (f32[512,32]{0,1:T(8,128)S(1)}, f32[512,32]{0,1:T(8,128)}, u32[]{:S(2)}) copy-start(f32[512,32]{0,1:T(8,128)} %get-tuple-element.438) | copy-start | bytes 196612
  347.3 3.8 copy-start.31
  356.8 3.8 copy-start.31
  366.3 3.8 copy-start.31
  375.8 3.8 copy-start.31
  385.3 3.8 copy-start.31
  394.9 3.8 copy-start.31
  401.9 4.3 copy-start.48
  402.2 4.1 copy-start.50
  406.2 181.1 %reduce-scatter.8.cloned.1.call-start = ((), (), s32[]{:S(2)}) async-start(), calls=%async_computation.11 | async-start | bytes 4718592 | tf_op jit(solution)/shard_map/reduce_scatter | solution.py:279
  412.2 3.0 copy-start.39
  412.2 3.0 copy-start.44
  412.2 214.5 %reduce-scatter.16.cloned.1.call-start = ((), (), s32[]{:S(2)}) async-start(), calls=%async_computation.15 | async-start | bytes 1253376 | tf_op jit(solution)/shard_map/reduce_scatter | solution.py:328
  415.1 273.0 %reduce-scatter.14.cloned.1.call-start = ((), (), s32[]{:S(2)}) async-start(), calls=%async_computation.14 | async-start | bytes 1253376 | tf_op jit(solution)/shard_map/reduce_scatter | solution.py:326
  417.0 3.4 copy-start.8
  417.0 3.4 copy-start.77
  417.0 3.4 copy-start.100
  417.0 332.4 %reduce-scatter.12.cloned.1.call-start = ((), (), s32[]{:S(2)}) async-start(), calls=%async_computation.13 | async-start | bytes 1253376 | tf_op jit(solution)/shard_map/reduce_scatter | solution.py:325
  420.3 408.2 %reduce-scatter.18.cloned.1.call-start = ((), (), s32[]{:S(2)}) async-start(), calls=%async_computation.16 | async-start | bytes 5013504 | tf_op jit(solution)/shard_map/reduce_scatter | solution.py:329
  425.6 482.0 %reduce-scatter.20.cloned.1.call-start = ((), (), s32[]{:S(2)}) async-start(), calls=%async_computation.17 | async-start | bytes 5013504 | tf_op jit(solution)/shard_map/reduce_scatter | solution.py:330
  431.8 547.7 %reduce-scatter.10.cloned.1.call-start = ((), (), s32[]{:S(2)}) async-start(), calls=%async_computation.12 | async-start | bytes 3760128 | tf_op jit(solution)/shard_map/reduce_scatter | solution.py:324
  437.1 7.5 copy-start.85
  437.2 7.5 copy-start.84
  439.5 5.2 copy-start.49
  444.7 76.1 %copy-start.80 = (f32[768]{0:T(1024)S(1)}, f32[768]{0:T(1024)}, u32[]{:S(2)}) copy-start(f32[768]{0:T(1024)} %get-tuple-element.401) | copy-start | bytes 9220
  444.7 76.1 %copy-start.81 = (f32[768]{0:T(1024)S(1)}, f32[768]{0:T(1024)}, u32[]{:S(2)}) copy-start(f32[768]{0:T(1024)} %get-tuple-element.431) | copy-start | bytes 9220
  444.7 76.1 %copy-start.88 = (f32[1536]{0:T(1024)S(1)}, f32[1536]{0:T(1024)}, u32[]{:S(2)}) copy-start(f32[1536]{0:T(1024)} %get-tuple-element.398) | copy-start | bytes 18436
  444.7 137.8 %copy-start.72 = (f32[512]{0:T(512)S(1)}, f32[512]{0:T(512)}, u32[]{:S(2)}) copy-start(f32[512]{0:T(512)} %copy-done.71) | copy-start | bytes 6148
  586.4 393.0 %copy-start.1 = (bf16[1536,768]{1,0:T(8,128)(2,1)S(1)}, bf16[1536,768]{1,0:T(8,128)(2,1)}, u32[]{:S(2)}) copy-start(bf16[1536,768]{1,0:T(8,128)(2,1)} %param.46) | copy-start | bytes 7077892
  (71 other events, 104.5 us)
Sparse Core Ops, SparseCore 0:
  54.3 54.2 all-reduce.10
  133.5 51.5 all-reduce.12
  204.2 51.5 all-reduce.14
  276.9 51.5 all-reduce.16
  332.5 98.9 all-reduce.18
  433.7 84.8 all-reduce.20
  520.8 43.4 reduce-scatter.7
  568.5 58.1 reduce-scatter.15
  630.9 57.1 reduce-scatter.13
  692.2 57.1 reduce-scatter.11
  753.9 74.5 reduce-scatter.17
  832.7 74.7 reduce-scatter.19
  912.0 67.3 reduce-scatter.9
where the time goes:
time: 995 us; the launch traced here: 986 us
  waiting for transfers between devices  580 us (58%)
  matrix products  152 us (15%)
  local copies, waits for them, and re-layouts  117 us (12%)
  blocking collectives  61.8 us (6%)
  other arithmetic  57.1 us (6%)
  between operations  16.9 us (2%)
    reduce_scatter x1, waiting for transfers between devices, per_device(): lax.psum_scatter(mlp_out_w_grad, 'dp', scatter_dimension=1, tiled=True)  79.1 us
    reduce_scatter x1, waiting for transfers between devices, per_device(): lax.psum_scatter(mlp_in_w_grad, 'dp', scatter_dimension=0, tiled=True)  79 us
    psum x1, waiting for transfers between devices, per_device(): lax.psum(jnp.dot(act_low, mlp_out_w, preferred_element_type=jnp.float32),...  72.7 us
    reduce_scatter x1, waiting for transfers between devices, per_device(): lax.psum_scatter(self_qkv_w_grad, 'dp', scatter_dimension=0, tiled=True)  71.9 us
    psum x1, blocking collectives, per_device(): lax.psum((gain_grads, shift_grads, self_qkv_b_grad, self_out_b_grad, cros...  61.8 us
    reduce_scatter x1, waiting for transfers between devices, per_device(): lax.psum_scatter(cross_q_w_grad, 'dp', scatter_dimension=0, tiled=True)  61.4 us
    reduce_scatter x1, waiting for transfers between devices, per_device(): lax.psum_scatter(self_out_w_grad, 'dp', scatter_dimension=1, tiled=True)  61.3 us
    psum x1, waiting for transfers between devices, per_device(): lax.psum(jnp.dot(cross_mix, cross_out_w, preferred_element_type=jnp.float...  50.7 us
  transfers between devices with their start and end apart: 13, of which 10 were waited for; matrix products, arithmetic and copies ran while one was open for 21% of the time, Pallas kernels for 0%

commit v1 on v0

--- a/solution.py
+++ b/solution.py
@@ -195,7 +195,11 @@
     act, gelu_pull = jax.vjp(exact_gelu, pre_act)
     act_low = act.astype(jnp.bfloat16)
     mlp = (
-        lax.psum(jnp.dot(act_low, mlp_out_w, preferred_element_type=jnp.float32), "tp") + mlp_out_b
+        jnp.sum(
+            lax.all_gather(jnp.dot(act_low, mlp_out_w, preferred_element_type=jnp.float32), "tp"),
+            axis=0,
+        )
+        + mlp_out_b
     )
     output = lax.dynamic_slice_in_dim(hidden_two + mlp, own_start, own_width, 1).astype(
         jnp.bfloat16

time: 995 us -> 1010 us (1.015)
  local copies, waits for them, and re-layouts: 117 us -> 128 us
  other arithmetic: 57.1 us -> 67.9 us
    psum x1, waiting for transfers between devices: 72.7 us -> 45.6 us  [per_device(): lax.psum(jnp.einsum('tcf,dcf->td', grad_qkv, self_qkv_w, preferred_elemen...]
    all_gather x0 -> x1, waiting for transfers between devices: none -> 10.7 us  [per_device(): lax.all_gather(jnp.dot(act_low, mlp_out_w, preferred_element_type=jnp.flo...]
    unnamed x226 -> x192, local copies, waits for them, and re-layouts: 23.9 us -> 20.9 us
  transfers between devices with their start and end apart: 13 -> 14, of which waited for: 10 -> 11; matrix products, arithmetic and copies ran while one was open for 21% -> 23% of each run, Pallas kernels for 0% -> 0%
where the time goes in v1:
time: 1010 us; the launch traced here: 1000 us
  waiting for transfers between devices  571 us (57%)
  matrix products  158 us (16%)
  local copies, waits for them, and re-layouts  128 us (13%)
  other arithmetic  67.9 us (7%)
  blocking collectives  61.8 us (6%)
  between operations  16.9 us (2%)
    reduce_scatter x1, waiting for transfers between devices, per_device(): lax.psum_scatter(mlp_out_w_grad, 'dp', scatter_dimension=1, tiled=True)  79.3 us
    reduce_scatter x1, waiting for transfers between devices, per_device(): lax.psum_scatter(mlp_in_w_grad, 'dp', scatter_dimension=0, tiled=True)  78.9 us
    reduce_scatter x1, waiting for transfers between devices, per_device(): lax.psum_scatter(self_qkv_w_grad, 'dp', scatter_dimension=0, tiled=True)  71.6 us
    psum x1, blocking collectives, per_device(): lax.psum((gain_grads, shift_grads, self_qkv_b_grad, self_out_b_grad, cros...  61.8 us
    reduce_scatter x1, waiting for transfers between devices, per_device(): lax.psum_scatter(self_out_w_grad, 'dp', scatter_dimension=1, tiled=True)  61.4 us
    reduce_scatter x1, waiting for transfers between devices, per_device(): lax.psum_scatter(cross_q_w_grad, 'dp', scatter_dimension=0, tiled=True)  61.3 us
    psum x1, waiting for transfers between devices, per_device(): lax.psum(jnp.dot(cross_mix, cross_out_w, preferred_element_type=jnp.float...  51.2 us
    psum x1, waiting for transfers between devices, per_device(): lax.psum(jnp.einsum('tf,df->td', grad_pre, mlp_in_w, preferred_element_ty...  48.9 us
  transfers between devices with their start and end apart: 14, of which 11 were waited for; matrix products, arithmetic and copies ran while one was open for 23% of the time, Pallas kernels for 0%

profile of v1, /device:TPU:0, one launch (start us, length us, event | category | flops | bytes accessed | tf_op | source)
XLA Modules:
  0.0 1004.8 jit_solution(11979706225787758646)
XLA Ops:
  11.8 2.8 convolution_add_fusion.1
  20.6 2.4 subtract_convert_fusion.2
  24.2 2.2 copy.158
  28.2 2.2 copy.159
  30.4 20.7 %while.30 = (s32[]{:T(128)}, bf16[6,512,64]{1,2,0:T(8,128)(2,1)S(1)}, f32[6,512,1]{1,2,0:T(1,128)}, bf16[6,512,64]{2,1,0:T(8,128)(2,1)}, bf16[6,512,64]{2,1,0:T(...) while((s32[]{:T(128)}, ...), condition=%wide.region_6.7_spmd.clone.clone, body=%wide.region_3.6_spmd.clone.sunk.clone | while | flops 70254080 | bytes 3701353 | solution.py:151
  51.1 3.0 fusion.123
  55.0 4.3 add_convert_fusion.1
  59.3 2.8 copy.162
  65.7 4.0 gather_fusion
  69.7 6.0 copy.165
  75.8 5.7 reshape.384
  81.4 3.9 fusion.120
  85.3 23.2 %all-reduce.10.cloned.1.call-done = f32[512,768]{1,0:T(8,128)} async-done(((f32[512,768]{1,0:T(8,128)}), f32[512,768]{1,0:T(8,128)}) %all-reduce.10.cloned.1.call-update) | async-done | bytes 1572880 | tf_op jit(solution)/shard_map/psum | solution.py:156
  114.4 2.3 copy.181
  116.7 2.8 multiply_reduce_fusion.2
  122.1 2.4 convolution_bitcast_fusion.6
  126.6 2.6 reshape.386
  133.7 51.2 %all-reduce.12.cloned.1.call-done = f32[512,768]{1,0:T(8,128)} async-done(((f32[512,768]{1,0:T(8,128)}), f32[512,768]{1,0:T(8,128)}) %all-reduce.12.cloned.1.call-update) | async-done | bytes 1572880 | tf_op jit(solution)/shard_map/psum | solution.py:189
  184.9 2.3 fusion.117
  189.9 10.2 %convert_reduce_fusion = (f32[1536]{0:T(1024)}, bf16[512,1536]{1,0:T(8,128)(2,1)S(1)}, f32[512,1536]{1,0:T(8,128)}) fusion(f32[512,1536]{1,0:T(8,128)S(1)} %convolution_add_fusion, bf16[512,768]{1,0:T(8,128)(2,1)S(1)} %copy-done.15, bf16[1536,768]{1,0:T(8,128)(2,1)S(1)} %copy-done), kind=kOutput, calls=%fused_computation.61 | convolution fusion | flops 1266153984 | bytes 11016192 | tf_op jit(solution)/shard_map/td,fd->tf/dot_general | solution.py:210
  201.3 2.6 fusion.125
  206.6 48.9 %all-reduce.14.cloned.1.call-done = f32[512,768]{1,0:T(8,128)} async-done(((f32[512,768]{1,0:T(8,128)}), f32[512,768]{1,0:T(8,128)}) %all-reduce.14.cloned.1.call-update) | async-done | bytes 1572880 | tf_op jit(solution)/shard_map/psum | solution.py:214
  255.6 3.2 multiply_reduce_fusion.3
  263.5 2.3 concatenate.39
  267.5 3.7 multiply_reduce_fusion.1
  273.7 2.2 multiply_bitcast_fusion
  279.9 3.0 fusion.84
  283.2 3.4 convolution_bitcast_fusion.2
  286.6 3.4 pad_maximum_fusion
  290.0 13.6 %copy.183 = f32[8,256,2,6,64]{4,3,2,1,0:T(8,128)} copy(f32[8,256,2,6,64]{1,4,3,0,2:T(8,128)} %pad_maximum_fusion) | data formatting | bytes 12582912 | tf_op jit(solution)/shard_map/stack | solution.py:265
  303.6 14.9 %reshape.389 = f32[16,98304]{1,0:T(8,128)} reshape(f32[8,256,2,6,64]{4,3,2,1,0:T(8,128)} %copy.183) | data formatting | bytes 12582912 | tf_op jit(solution)/shard_map/reshape | solution.py:265
  318.5 6.3 convolution_convert_fusion
  324.8 3.9 convert_element_type.173
  328.7 4.7 convolution_bitcast_fusion.4
  333.4 5.3 copy.188
  338.8 3.6 multiply_convert_fusion.2
  343.6 2.5 fusion.124
  346.4 3.2 multiply_reduce_fusion.4
  355.4 2.2 copy.174
  357.6 57.2 %while.31 = (s32[]{:T(128)}, f32[6,512,64]{1,2,0:T(8,128)}, f32[6,512,64]{1,2,0:T(8,128)}, bf16[6,512,64]{1,2,0:T(8,128)(2,1)}, bf16[6,512,64]{2,1,0:T(8,128)(2,...) while((s32[]{:T(128)}, f32[6,512,64]{1,2,0:T(8,128)}, ...), condition=%wide.region_25.26_spmd.clone.clone, body=%wide.region_23.25_spmd.clone.sunk.clone | while | flops 171245056 | bytes 12345017 | solution.py:300
  416.7 2.4 subtract_convert_fusion.1
  425.5 4.3 convolution_bitcast_fusion.5
  429.9 4.9 convolution_bitcast_fusion.3
  434.9 3.0 fusion.81
  438.0 3.0 fusion.83
  441.1 3.2 fusion.108
  444.3 6.0 fusion.111
  450.4 5.2 fusion.126
  456.3 4.4 fusion.78
  467.0 4.1 fusion.62
  472.7 10.7 %all-gather.3.cloned.1.call-done = f32[1024,768]{1,0:T(8,128)} async-done(((f32[512,768]{1,0:T(8,128)}), f32[1024,768]{1,0:T(8,128)}) %all-gather.3.cloned.1.call-update) | async-done | bytes 3145744 | tf_op jit(solution)/shard_map/all_gather | solution.py:199
  483.4 3.4 reduce_sum.290
  489.3 2.2 fusion.75
  491.6 45.6 %all-reduce.18.cloned.1.call-done = f32[512,768]{1,0:T(8,128)} async-done(((f32[512,768]{1,0:T(8,128)}), f32[512,768]{1,0:T(8,128)}) %all-reduce.18.cloned.1.call-update) | async-done | bytes 1572880 | tf_op jit(solution)/shard_map/psum | solution.py:312
  537.3 2.1 fusion.59
  539.5 61.8 %all-reduce.2 = (f32[3,768]{1,0:T(4,128)}, f32[3,768]{1,0:T(4,128)}, f32[3,384]{1,0:T(4,128)}, f32[768]{0:T(1024)}, f32[384]{0:T(512)}, /*index=5*/f32[384]{0:T(...) all-reduce(f32[3,768]{1,0:T(4,128)S(1)} %pad_maximum_fusion.12, ...), channel_id=1, replica_groups=mesh['dp'=16,'tp'=2] {'dp'}, use_global_device_ids=true, to_apply=%region_33.34 | all-reduce | flops 10368 | bytes 82944 | tf_op jit(solution)/shard_map/psum | solution.py:348
  601.3 2.2 fusion.114
  604.5 2.4 convert_element_type.169
  606.9 38.5 %reduce-scatter.16.cloned.1.call-done = f32[384,48]{0,1:T(8,128)} async-done(((f32[384,768]{0,1:T(8,128)}), f32[384,48]{0,1:T(8,128)}) %reduce-scatter.16.cloned.1.call-update) | async-done | bytes 73744 | tf_op jit(solution)/shard_map/reduce_scatter | solution.py:332
  645.4 61.3 %reduce-scatter.14.cloned.1.call-done = f32[48,384]{1,0:T(8,128)} async-done(((f32[768,384]{1,0:T(8,128)}), f32[48,384]{1,0:T(8,128)}) %reduce-scatter.14.cloned.1.call-update) | async-done | bytes 73744 | tf_op jit(solution)/shard_map/reduce_scatter | solution.py:330
  706.7 61.4 %reduce-scatter.12.cloned.1.call-done = f32[384,48]{0,1:T(8,128)} async-done(((f32[384,768]{0,1:T(8,128)}), f32[384,48]{0,1:T(8,128)}) %reduce-scatter.12.cloned.1.call-update) | async-done | bytes 73744 | tf_op jit(solution)/shard_map/reduce_scatter | solution.py:329
  768.1 78.9 %reduce-scatter.18.cloned.1.call-done = f32[48,1536]{1,0:T(8,128)} async-done(((f32[768,1536]{1,0:T(8,128)}), f32[48,1536]{1,0:T(8,128)}) %reduce-scatter.18.cloned.1.call-update) | async-done | bytes 294928 | tf_op jit(solution)/shard_map/reduce_scatter | solution.py:333
  847.0 79.3 %reduce-scatter.20.cloned.1.call-done = f32[1536,48]{0,1:T(8,128)} async-done(((f32[1536,768]{0,1:T(8,128)}), f32[1536,48]{0,1:T(8,128)}) %reduce-scatter.20.cloned.1.call-update) | async-done | bytes 294928 | tf_op jit(solution)/shard_map/reduce_scatter | solution.py:334
  926.2 71.6 %reduce-scatter.10.cloned.1.call-done = f32[48,3,384]{2,0,1:T(8,128)} async-done(((f32[768,3,384]{2,0,1:T(8,128)}), f32[48,3,384]{2,0,1:T(8,128)}) %reduce-scatter.10.cloned.1.call-update) | async-done | bytes 221200 | tf_op jit(solution)/shard_map/reduce_scatter | solution.py:328
  (406 shorter events, 156.2 us)
Async XLA Ops:
  7.2 182.7 %copy-start = (bf16[1536,768]{1,0:T(8,128)(2,1)S(1)}, bf16[1536,768]{1,0:T(8,128)(2,1)}, u32[]{:S(2)}) copy-start(bf16[1536,768]{1,0:T(8,128)(2,1)} %param.46) | copy-start | bytes 7077892
  7.2 101.3 %all-reduce.10.cloned.1.call-start = ((), (), s32[]{:S(2)}) async-start(), calls=%async_computation.7 | async-start | bytes 3145728 | tf_op jit(solution)/shard_map/psum | solution.py:156
  8.7 10.3 %copy-start.24 = (bf16[6,512,64]{1,2,0:T(8,128)(2,1)}, bf16[6,512,64]{1,2,0:T(8,128)(2,1)S(1)}, u32[]{:S(2)}) copy-start(bf16[6,512,64]{1,2,0:T(8,128)(2,1)S(1)} %fusion.122) | copy-start | bytes 1179652
  10.2 4.5 copy-start.46
  11.1 3.5 copy-start.54
  18.3 4.7 copy-start.52
  24.2 6.2 copy-start.28
  24.2 6.2 copy-start.77
  51.1 3.8 copy-start.82
  54.1 130.8 %all-reduce.12.cloned.1.call-start = ((), (), s32[]{:S(2)}) async-start(), calls=%async_computation.8 | async-start | bytes 3145728 | tf_op jit(solution)/shard_map/psum | solution.py:189
  81.4 27.1 %copy-start.88 = (f32[768]{0:T(1024)S(1)}, f32[768]{0:T(1024)}, u32[]{:S(2)}) copy-start(f32[768]{0:T(1024)} %param.37) | copy-start | bytes 9220
  119.5 86.5 %copy-start.41 = (f32[8,6,64]{2,1,0:T(8,128)}, f32[8,6,64]{2,1,0:T(8,128)S(1)}, u32[]{:S(2)}) copy-start(f32[8,6,64]{2,1,0:T(8,128)S(1)} %get-tuple-element.441) | copy-start | bytes 36868
  120.6 85.4 %copy-start.43 = (f32[8,6,64]{2,1,0:T(8,128)}, f32[8,6,64]{2,1,0:T(8,128)S(1)}, u32[]{:S(2)}) copy-start(f32[8,6,64]{2,1,0:T(8,128)S(1)} %fusion.50) | copy-start | bytes 36868
  131.2 53.7 %copy-start.81 = (f32[768]{0:T(1024)S(1)}, f32[768]{0:T(1024)}, u32[]{:S(2)}) copy-start(f32[768]{0:T(1024)} %param.43) | copy-start | bytes 9220
  133.2 122.3 %all-reduce.14.cloned.1.call-start = ((), (), s32[]{:S(2)}) async-start(), calls=%async_computation.9 | async-start | bytes 3145728 | tf_op jit(solution)/shard_map/psum | solution.py:214
  184.9 3.4 copy-start.90
  187.5 71.3 %copy-start.57 = (f32[512]{0:T(512)}, f32[512]{0:T(512)S(1)}, u32[]{:S(2)}) copy-start(f32[512]{0:T(512)S(1)} %fusion.101) | copy-start | bytes 6148
  189.9 10.2 %copy-start.30 = (f32[512,1536]{1,0:T(8,128)}, f32[512,1536]{1,0:T(8,128)S(1)}, u32[]{:S(2)}) copy-start(f32[512,1536]{1,0:T(8,128)S(1)} %convolution_add_fusion) | copy-start | bytes 9437188
  203.9 142.5 %all-reduce.16.cloned.1.call-start = ((), (), s32[]{:S(2)}) async-start(), calls=%async_computation.10 | async-start | bytes 3145728 | tf_op jit(solution)/shard_map/psum | solution.py:286
  255.6 3.3 copy-start.6
  255.6 3.3 copy-start.20
  263.5 3.6 copy-start.42
  267.4 3.7 copy-start.29
  267.5 3.7 copy-start.4
  282.9 188.2 %all-reduce.20.cloned.1.call-start = ((), (), s32[]{:S(2)}) async-start(), calls=%async_computation.20 | async-start | bytes 4718592
  283.1 3.4 copy-start.12
  338.8 144.6 %all-gather.3.cloned.1.call-start = ((), (), s32[]{:S(2)}) async-start(), calls=%async_computation.19 | async-start | bytes 4718592 | tf_op jit(solution)/shard_map/all_gather | solution.py:199
  346.1 191.1 %all-reduce.18.cloned.1.call-start = ((), (), s32[]{:S(2)}) async-start(), calls=%async_computation.11 | async-start | bytes 3145728 | tf_op jit(solution)/shard_map/psum | solution.py:312
  346.4 3.9 copy-start.2
  346.4 3.9 copy-start.19
  354.2 3.4 copy-start.78
  354.2 3.4 copy-start.89
  363.3 3.8 copy-start.26
  372.9 3.8 copy-start.26
  382.4 3.8 copy-start.26
  391.9 3.8 copy-start.26
  401.5 3.8 copy-start.26
  411.0 3.8 copy-start.26
  429.8 174.6 %reduce-scatter.8.cloned.1.call-start = ((), (), s32[]{:S(2)}) async-start(), calls=%async_computation.12 | async-start | bytes 4718592 | tf_op jit(solution)/shard_map/reduce_scatter | solution.py:283
  434.9 210.5 %reduce-scatter.16.cloned.1.call-start = ((), (), s32[]{:S(2)}) async-start(), calls=%async_computation.16 | async-start | bytes 1253376 | tf_op jit(solution)/shard_map/reduce_scatter | solution.py:332
  437.9 268.7 %reduce-scatter.14.cloned.1.call-start = ((), (), s32[]{:S(2)}) async-start(), calls=%async_computation.15 | async-start | bytes 1253376 | tf_op jit(solution)/shard_map/reduce_scatter | solution.py:330
  441.0 3.3 copy-start.58
  441.0 3.3 copy-start.87
  441.0 327.1 %reduce-scatter.12.cloned.1.call-start = ((), (), s32[]{:S(2)}) async-start(), calls=%async_computation.14 | async-start | bytes 1253376 | tf_op jit(solution)/shard_map/reduce_scatter | solution.py:329
  444.3 402.7 %reduce-scatter.18.cloned.1.call-start = ((), (), s32[]{:S(2)}) async-start(), calls=%async_computation.17 | async-start | bytes 5013504 | tf_op jit(solution)/shard_map/reduce_scatter | solution.py:333
  450.4 475.9 %reduce-scatter.20.cloned.1.call-start = ((), (), s32[]{:S(2)}) async-start(), calls=%async_computation.18 | async-start | bytes 5013504 | tf_op jit(solution)/shard_map/reduce_scatter | solution.py:334
  455.7 542.2 %reduce-scatter.10.cloned.1.call-start = ((), (), s32[]{:S(2)}) async-start(), calls=%async_computation.13 | async-start | bytes 3760128 | tf_op jit(solution)/shard_map/reduce_scatter | solution.py:328
  460.8 3.3 copy-start.65
  460.8 3.9 copy-start.64
  483.4 3.5 copy-start.67
  483.4 4.0 copy-start.66
  483.4 4.6 copy-start.35
  489.3 47.9 %copy-start.56 = (f32[512]{0:T(512)S(1)}, f32[512]{0:T(512)}, u32[]{:S(2)}) copy-start(f32[512]{0:T(512)} %copy-done.54) | copy-start | bytes 6148
  491.5 47.8 %copy-start.69 = (f32[1,768]{1,0:T(1,128)S(1)}, f32[1,768]{1,0:T(1,128)}, u32[]{:S(2)}) copy-start(f32[1,768]{1,0:T(1,128)} %reshape.392) | copy-start | bytes 9220
  491.5 47.8 %copy-start.71 = (f32[1,768]{1,0:T(1,128)S(1)}, f32[1,768]{1,0:T(1,128)}, u32[]{:S(2)}) copy-start(f32[1,768]{1,0:T(1,128)} %reshape.391) | copy-start | bytes 9220
  491.5 47.9 %copy-start.68 = (f32[1,768]{1,0:T(1,128)S(1)}, f32[1,768]{1,0:T(1,128)}, u32[]{:S(2)}) copy-start(f32[1,768]{1,0:T(1,128)} %reshape.395) | copy-start | bytes 9220
  491.6 47.9 %copy-start.70 = (f32[1,768]{1,0:T(1,128)S(1)}, f32[1,768]{1,0:T(1,128)}, u32[]{:S(2)}) copy-start(f32[1,768]{1,0:T(1,128)} %reshape.394) | copy-start | bytes 9220
  491.6 47.9 %copy-start.61 = (f32[768]{0:T(1024)S(1)}, f32[768]{0:T(1024)}, u32[]{:S(2)}) copy-start(f32[768]{0:T(1024)} %get-tuple-element.399) | copy-start | bytes 9220
  491.6 47.9 %copy-start.62 = (f32[768]{0:T(1024)S(1)}, f32[768]{0:T(1024)}, u32[]{:S(2)}) copy-start(f32[768]{0:T(1024)} %get-tuple-element.401) | copy-start | bytes 9220
  491.6 47.9 %copy-start.63 = (f32[768]{0:T(1024)S(1)}, f32[768]{0:T(1024)}, u32[]{:S(2)}) copy-start(f32[768]{0:T(1024)} %get-tuple-element.429) | copy-start | bytes 9220
  491.6 47.9 %copy-start.72 = (f32[384]{0:T(512)S(1)}, f32[384]{0:T(512)}, u32[]{:S(2)}) copy-start(f32[384]{0:T(512)} %convert_reduce_fusion.6) | copy-start | bytes 4612
  491.6 47.9 %copy-start.73 = (f32[384]{0:T(512)S(1)}, f32[384]{0:T(512)}, u32[]{:S(2)}) copy-start(f32[384]{0:T(512)} %fusion.62) | copy-start | bytes 4612
  491.6 47.9 %copy-start.75 = (f32[1536]{0:T(1024)S(1)}, f32[1536]{0:T(1024)}, u32[]{:S(2)}) copy-start(f32[1536]{0:T(1024)} %get-tuple-element.396) | copy-start | bytes 18436
  491.6 109.7 %copy-start.50 = (f32[512]{0:T(512)S(1)}, f32[512]{0:T(512)}, u32[]{:S(2)}) copy-start(f32[512]{0:T(512)} %copy-done.49) | copy-start | bytes 6148
  (55 other events, 81.5 us)
Sparse Core Ops, SparseCore 0:
  54.2 54.2 all-reduce.9
  133.3 51.5 all-reduce.11
  204.0 51.5 all-reduce.13
  283.0 51.5 all-reduce.15
  338.9 99.5 all-reduce.19
  439.9 43.4 all-gather.2
  485.7 51.5 all-reduce.17
  539.5 43.4 reduce-scatter.7
  587.2 58.1 reduce-scatter.15
  649.4 57.1 reduce-scatter.13
  710.9 57.1 reduce-scatter.11
  772.4 74.5 reduce-scatter.17
  851.4 74.7 reduce-scatter.19
  930.5 67.2 reduce-scatter.9
